TPU v7x, 32 devices: a whole 2x2x4 slice. The times are simulated.
32 devices in a mesh: row: 4 (over y, x), col: 4 (over z), vox: 2 (over core).
Axes of the slice: x: 2, y: 2, z: 4, core: 2. Of those that a mesh axis runs over, the one named last changes fastest.
Arguments:
- coeffs_r: bfloat16 [32, 4, 64, 2, 1024], P(None, 'row', None, None, 'col'), may hold values from -0.125 to 0.125
- rhs: bfloat16 [32, 4, 64, 1536], P('col', 'row', None, 'vox'), may hold values from -6 to 6
- inverses: bfloat16 [2, 1024, 1024], replicated, may hold values from -0.1875 to 0.1875
Outputs:
- updated: bfloat16 [32, 4, 64, 1536], P('col', 'row', None, 'vox')
All inputs are finite; a program needn't handle non-finite values.
Results may differ from a plain program's by a relative error of at most 0.0049.
Values may be sent and summed in bfloat16 or wider, within the bound.
No kernel may reach another device: no remote copies, remote signals or barrier semaphores. Data moves between devices by JAX's collectives and lax.ppermute only.
A program may use at most 64 MiB of HBM per device.

v0:
```python
import functools

import jax
import jax.numpy as jnp
from jax import lax
from jax.experimental import pallas as pl
from jax.experimental.pallas import tpu as pltpu
from jax.sharding import PartitionSpec as P

VMEM = pl.BlockSpec(memory_space=pltpu.VMEM)
CHUNKS = 2
SMEM = pl.BlockSpec(memory_space=pltpu.SMEM)


def chunk_bounds(voxels):
    cut = voxels // 256 * 2 // 3 * 256 or voxels // 2
    return [slice(0, cut), slice(cut, voxels)]


def dot(a, b):
    return jnp.dot(a, b, preferred_element_type=jnp.float32)


def assemble(full, pieces, row_pos, rows):
    count = len(pieces)
    tail = pieces[0].shape[0] // rows
    for d, piece in enumerate(pieces):
        p = row_pos ^ d
        for k in range(tail):
            at = pl.multiple_of((k * count + p) * rows, rows)
            full[pl.ds(at, rows), :] = piece[k * rows : (k + 1) * rows, :]


def solve(x, inverses, which, full):
    step = min(256, x.shape[0])

    def body(m, _):
        at = pl.multiple_of(m * step, step)
        x[pl.ds(at, step), :] = dot(inverses[which, pl.ds(at, step), :], full[...]).astype(x.dtype)
        return 0

    lax.fori_loop(0, x.shape[0] // step, body, 0)


def mid_kernel(row_count, rows, start, cols, where, *refs):
    pieces = [ref.at[:, cols] for ref in refs[:row_count]]
    inverses, mine, other, mid, out, full, x = refs[row_count:]
    assemble(full, pieces, where[0], rows)
    solve(x, inverses, 1, full)
    half, piece = mine.shape[1], mid.shape[0]
    for h in range(2):
        low, high = max(start, h * half), min(start + piece, (h + 1) * half)
        if low >= high:
            continue
        to = slice(low - start, high - start)

        def rest(coeffs):
            total = mid[to, cols].astype(jnp.float32)
            total = subtract(total, coeffs, x, slice(low - h * half, high - h * half))
            out[to, :] = total.astype(out.dtype)

        pl.when(where[1] == h)(functools.partial(rest, mine))
        pl.when(where[1] != h)(functools.partial(rest, other))


def subtract(total, coeffs, x, at):
    own = coeffs.shape[2]
    for c in range(coeffs.shape[0]):
        total = total - dot(coeffs[c, at, :], x[c * own : (c + 1) * own, :])
    return total


def own_rows(x, row_pos, count, rows):
    tail = x.shape[0] // (count * rows)
    return [x[pl.ds(pl.multiple_of((k * count + row_pos) * rows, rows), rows), :] for k in range(tail)]


def last_kernel(row_count, rows, where, *refs):
    pieces = refs[:row_count]
    inverses, mine, other, rhs, acc, x_rows, full, x = refs[row_count:]
    assemble(full, pieces, where[0], rows)
    solve(x, inverses, 1, full)
    for k, part in enumerate(own_rows(x, where[0], row_count, rows)):
        x_rows[k * rows : (k + 1) * rows, :] = part
    half = mine.shape[1]
    for coeffs, h in ((mine, where[1]), (other, 1 - where[1])):
        at = pl.multiple_of(h * half, half)
        total = rhs[pl.ds(at, half), :].astype(jnp.float32)
        acc[pl.ds(at, half), :] = subtract(total, coeffs, x, slice(None))


def final_kernel(row_count, rows, chunks, where, *refs):
    pieces = refs[: row_count * chunks]
    inverses, mine, other, acc, x_rows, out, full, x = refs[row_count * chunks :]
    for n, cols in enumerate(chunk_bounds(full.shape[1])):
        assemble(full.at[:, cols], pieces[n::chunks], where[0], rows)
    solve(x, inverses, 0, full)
    half = mine.shape[1]
    for coeffs, h in ((mine, where[1]), (other, 1 - where[1])):
        at = pl.multiple_of(h * half, half)
        total = subtract(acc[pl.ds(at, half), :], coeffs, x, slice(None))
        out[pl.ds(at, half), :] = total.astype(out.dtype)

    @pl.when(where[2] == 1)
    def _():
        piece = x_rows.shape[0]
        start = out.shape[0] - 2 * piece
        for k, part in enumerate(own_rows(x, where[0], row_count, rows)):
            out[start + k * rows : start + (k + 1) * rows, :] = part
        out[start + piece :, :] = x_rows[...]


def local(coeffs_r, rhs, inverses):
    row_count = lax.axis_size("row")
    col_count = lax.axis_size("col")
    vox_count = lax.axis_size("vox")
    row_pos = lax.axis_index("row")
    col_pos = lax.axis_index("col")
    vox_pos = lax.axis_index("vox")
    per_col = rhs.shape[0]
    rows = rhs.shape[2]
    voxels = rhs.shape[3]
    own = coeffs_r.shape[4]
    order = inverses.shape[1]
    tail = order // (rows * row_count)
    piece = tail * rows
    owner = col_count - 1
    where = jnp.stack([row_pos, vox_pos, (col_pos == owner).astype(jnp.int32)]).astype(jnp.int32)
    bf16 = jnp.bfloat16

    def gather_rows(value):
        pairs = [[(r, r ^ d) for r in range(row_count)] for d in range(row_count)]
        return [value] + [lax.ppermute(value, "row", pairs[d]) for d in range(1, row_count)]

    def step_down(value, step):
        stride = col_count >> (step + 1)
        targets = range(stride - 1, owner, 2 * stride)
        pairs = [(t + stride, t) for t in targets]
        if stride == 1:
            pairs += [(t, t + stride) for t in targets]
        got = lax.ppermute(value, "col", pairs)
        is_target = functools.reduce(jnp.logical_or, [col_pos == t for t in targets])
        return jnp.where(is_target, got, value)

    half = per_col // vox_count
    split = coeffs_r.reshape(col_count, vox_count, half * rows, 2, own)
    halves = lax.dynamic_slice_in_dim(split, vox_pos, 1, 1)[:, 0].transpose(2, 0, 1, 3)

    def spread_coeffs(which):
        return lax.all_to_all(halves[which], "col", 0, 0, tiled=True)

    def swap(value):
        return lax.ppermute(value, "vox", [(0, 1), (1, 0)])

    def scratch(width):
        return [pltpu.VMEM((order, width), bf16), pltpu.VMEM((order, width), bf16)]

    params = pltpu.CompilerParams(vmem_limit_bytes=12 << 20)

    def cost(width, n_rows):
        flops = 2 * order * width * (order + n_rows)
        return pl.CostEstimate(flops=flops, bytes_accessed=flops // 400, transcendentals=0)

    downs = col_count.bit_length() - 1
    mid_piece = rhs[per_col - 2 * tail : per_col - tail].reshape(piece, voxels)
    last_piece = rhs[per_col - tail :].reshape(piece, voxels)

    top = gather_rows(last_piece)
    spread = step_down(last_piece, 0)
    mine_1 = spread_coeffs(1)
    for s in range(1, downs):
        spread = step_down(spread, s)
    other_1 = swap(mine_1)

    mids = []
    for cols in chunk_bounds(voxels):
        width = cols.stop - cols.start
        mids.append(
            pl.pallas_call(
                functools.partial(mid_kernel, row_count, rows, (per_col - 2 * tail) * rows, cols),
                out_shape=jax.ShapeDtypeStruct((piece, width), bf16),
                in_specs=[SMEM] + [VMEM] * (row_count + 4),
                out_specs=VMEM,
                scratch_shapes=scratch(width),
                compiler_params=params,
                cost_estimate=cost(width, piece),
            )(where, *top, inverses, mine_1, other_1, mid_piece)
        )
    mids = [step_down(mid, 0) for mid in mids]
    last = gather_rows(spread)
    for s in range(1, downs):
        mids = [step_down(mid, s) for mid in mids]
    mine_0 = spread_coeffs(0)
    middle = [gather_rows(mid) for mid in mids]
    other_0 = swap(mine_0)

    flat = rhs.reshape(per_col * rows, voxels)
    acc, x_rows = pl.pallas_call(
        functools.partial(last_kernel, row_count, rows),
        out_shape=(jax.ShapeDtypeStruct(flat.shape, jnp.float32), jax.ShapeDtypeStruct((piece, voxels), bf16)),
        in_specs=[SMEM] + [VMEM] * (row_count + 4),
        out_specs=(VMEM, VMEM),
        scratch_shapes=scratch(voxels),
        compiler_params=params,
        cost_estimate=cost(voxels, per_col * rows),
        name="last",
    )(where, *last, inverses, mine_1, other_1, flat)
    pieces = [middle[n][d] for d in range(row_count) for n in range(CHUNKS)]
    out = pl.pallas_call(
        functools.partial(final_kernel, row_count, rows, CHUNKS),
        out_shape=jax.ShapeDtypeStruct(flat.shape, bf16),
        in_specs=[SMEM] + [VMEM] * (row_count * CHUNKS + 5),
        out_specs=VMEM,
        scratch_shapes=scratch(voxels),
        compiler_params=params,
        cost_estimate=cost(voxels, per_col * rows),
        name="final",
    )(where, *pieces, inverses, mine_0, other_0, acc, x_rows)
    return out.reshape(rhs.shape)


def solution(mesh):
    placed = (P(None, "row", None, None, "col"), P("col", "row", None, "vox"), P())

    return jax.shard_map(
        local, mesh=mesh, in_specs=placed, out_specs=P("col", "row", None, "vox"), check_vma=False
    )
```

profile of v0, /device:TPU:21, one launch (start us, length us, event | category | flops | bytes accessed | tf_op | source)
XLA Modules:
  0.0 114.7 jit_solution(1289721769291028118)
XLA Ops:
  0.0 1.6 %copy-done = bf16[32,1,64,2,256]{4,3,2,1,0:T(2,128)(2,1)S(1)} copy-done((bf16[32,1,64,2,256]{4,3,2,1,0:T(2,128)(2,1)S(1)}, bf16[32,1,64,2,256]{4,3,2,1,0:T(2,128)(2,1)}, u32[]{:S(2)}) %copy-start) | copy-done | bytes 2097176
  3.3 16.0 %all_to_all.10.refs_5_ = bf16[4,256,256]{2,1,0:T(8,128)(2,1)S(1)} all-to-all(bf16[4,256,256]{2,1,0:T(8,128)(2,1)S(1)} %get-tuple-element.10), channel_id=1, replica_groups=mesh['row'=4,'col'=4,'vox'=2] {'col'}, dimensions={0} | all-to-all | bytes 1048576 | tf_op jit(solution)/shard_map/all_to_all | solution.py:150
  19.3 1.5 %collective-permute-start.3 = (bf16[4,256,256]{2,1,0:T(8,128)(2,1)S(1)}, bf16[4,256,256]{2,1,0:T(8,128)(2,1)}, u32[]{:S(2)}, u32[]{:S(2)}) collective-permute-start(bf16[4,256,256]{2,1,0:T(8,128)(2,1)S(1)} %all_to_all.10.refs_5_), channel_id=1, source_target_pairs={{0,1},{1,0},{2,3},{3,2},{4,5},{5,4},{6,7},{7,6},{8,9},{9,8},{10,11... | collective-permute-start | bytes 1572872 | tf_op jit(solution)/shard_map/ppermute | solution.py:153
  20.8 1.2 %collective-permute-start.2 = (bf16[256,768]{1,0:T(8,128)(2,1)S(1)}, bf16[256,768]{1,0:T(8,128)(2,1)}, u32[]{:S(2)}, u32[]{:S(2)}) collective-permute-start(bf16[256,768]{1,0:T(8,128)(2,1)S(1)} %bitcast.21), channel_id=1, source_target_pairs={{0,24},{8,16},{16,8},{24,0},{1,25},{9,17},{17,9},{25,1},{2,26},{10... | collective-permute-start | bytes 1179656 | tf_op jit(solution)/shard_map/ppermute | solution.py:133
  22.1 1.2 %collective-permute-start.1 = (bf16[256,768]{1,0:T(8,128)(2,1)S(1)}, bf16[256,768]{1,0:T(8,128)(2,1)}, u32[]{:S(2)}, u32[]{:S(2)}) collective-permute-start(bf16[256,768]{1,0:T(8,128)(2,1)S(1)} %bitcast.22), channel_id=1, source_target_pairs={{0,16},{8,24},{16,0},{24,8},{1,17},{9,25},{17,1},{25,9},{2,18},{10... | collective-permute-start | bytes 1179656 | tf_op jit(solution)/shard_map/ppermute | solution.py:133
  23.6 6.5 %all-to-all-start.1 = ((bf16[4,256,256]{2,1,0:T(8,128)(2,1)}), bf16[4,256,256]{2,1,0:T(8,128)(2,1)}, u32[]{:S(2)}, u32[]{:S(2)}) async-start(bf16[4,256,256]{2,1,0:T(8,128)(2,1)} %get-tuple-element.9), calls=%async_computation.1 | async-start | bytes 1048576 | tf_op jit(solution)/shard_map/all_to_all | solution.py:150
  30.1 1.4 %collective-permute-start.15 = (bf16[256,768]{1,0:T(8,128)(2,1)S(1)}, bf16[256,768]{1,0:T(8,128)(2,1)}, u32[]{:S(2)}, u32[]{:S(2)}) collective-permute-start(bf16[256,768]{1,0:T(8,128)(2,1)S(1)} %bitcast.24), channel_id=1, source_target_pairs={{6,2},{7,3},{14,10},{15,11},{22,18},{23,19},{30,26},{31,27}} | collective-permute-start | bytes 1179656 | tf_op jit(solution)/shard_map/ppermute | solution.py:141
  32.6 8.8 %collective-permute-done.1.refs_2_ = bf16[256,768]{1,0:T(8,128)(2,1)} collective-permute-done((bf16[256,768]{1,0:T(8,128)(2,1)S(1)}, bf16[256,768]{1,0:T(8,128)(2,1)}, u32[]{:S(2)}, u32[]{:S(2)}) %collective-permute-start.1) | collective-permute-done | bytes 393248 | tf_op jit(solution)/shard_map/ppermute | solution.py:133
  41.4 2.2 %copy-done.1 = bf16[2,1024,1024]{2,1,0:T(8,128)(2,1)S(1)} copy-done((bf16[2,1024,1024]{2,1,0:T(8,128)(2,1)S(1)}, bf16[2,1024,1024]{2,1,0:T(8,128)(2,1)}, u32[]{:S(2)}) %copy-start.1) | copy-done | bytes 4194328
  43.6 3.0 %shard_map.38 = bf16[256,256]{1,0:T(8,128)(2,1)S(1)} custom-call(s32[3]{0:T(128)S(1)} %pad_add_fusion.where, bf16[256,768]{1,0:T(8,128)(2,1)S(1)} %bitcast.25, bf16[256,768]{1,0:T(8,128)(2,1)} %collective-permute-done.refs_1_, bf16[256,768]{1,0:T(8,128)(2,1)} %collective-permute-done.1.refs_2_, bf16[256,768]{1,0:T(8,128)(2,1)} %collective-permute-done.2.refs_3_, ...), custom_call_target="tpu_custom_call" | custom-call | flops 671088640 | bytes 1677721 | tf_op jit(solution)/shard_map/pallas_call | solution.py:179
  46.6 1.3 %collective-permute-start.6 = (bf16[256,256]{1,0:T(8,128)(2,1)S(1)}, bf16[256,256]{1,0:T(8,128)(2,1)}, u32[]{:S(2)}, u32[]{:S(2)}) collective-permute-start(bf16[256,256]{1,0:T(8,128)(2,1)S(1)} %shard_map.38), channel_id=1, source_target_pairs={{6,2},{7,3},{14,10},{15,11},{22,18},{23,19},{30,26},{31,27}} | collective-permute-start | bytes 393224 | tf_op jit(solution)/shard_map/ppermute | solution.py:141
  47.9 4.4 %shard_map.37 = bf16[256,512]{1,0:T(8,128)(2,1)} custom-call(s32[3]{0:T(128)S(1)} %pad_add_fusion.where, bf16[256,768]{1,0:T(8,128)(2,1)S(1)} %bitcast.26, bf16[256,768]{1,0:T(8,128)(2,1)} %collective-permute-done.refs_1_, bf16[256,768]{1,0:T(8,128)(2,1)} %collective-permute-done.1.refs_2_, bf16[256,768]{1,0:T(8,128)(2,1)} %collective-permute-done.2.refs_3_, ...), custom_call_target="tpu_custom_call" | custom-call | flops 1342177280 | bytes 3355443 | tf_op jit(solution)/shard_map/pallas_call | solution.py:179
  52.3 1.4 %collective-permute-start.4 = (bf16[256,512]{1,0:T(8,128)(2,1)}, bf16[256,512]{1,0:T(8,128)(2,1)}, u32[]{:S(2)}, u32[]{:S(2)}) collective-permute-start(bf16[256,512]{1,0:T(8,128)(2,1)} %shard_map.37), channel_id=1, source_target_pairs={{6,2},{7,3},{14,10},{15,11},{22,18},{23,19},{30,26},{31,27}} | collective-permute-start | bytes 786440 | tf_op jit(solution)/shard_map/ppermute | solution.py:141
  53.8 4.3 %collective-permute-start.16 = (bf16[256,768]{1,0:T(8,128)(2,1)S(1)}, bf16[256,768]{1,0:T(8,128)(2,1)S(1)}, u32[]{:S(2)}, u32[]{:S(2)}) collective-permute-start(bf16[256,768]{1,0:T(8,128)(2,1)S(1)} %broadcast_select_fusion), channel_id=1, source_target_pairs={{2,0},{6,4},{0,2},{4,6},{3,1},{7,5},{1,3},{5,7},{10,8},{14,12},{8,... | collective-permute-start | bytes 1179656 | tf_op jit(solution)/shard_map/ppermute | solution.py:141
  60.2 3.6 %collective-permute-start.5 = (bf16[256,512]{1,0:T(8,128)(2,1)S(1)}, bf16[256,512]{1,0:T(8,128)(2,1)S(1)}, u32[]{:S(2)}, u32[]{:S(2)}) collective-permute-start(bf16[256,512]{1,0:T(8,128)(2,1)S(1)} %broadcast_select_fusion.2), channel_id=1, source_target_pairs={{2,0},{6,4},{0,2},{4,6},{3,1},{7,5},{1,3},{5,7},{10,8},{14,12},{8,... | collective-permute-start | bytes 786440 | tf_op jit(solution)/shard_map/ppermute | solution.py:141
  63.8 8.0 %collective-permute-done.16 = bf16[256,768]{1,0:T(8,128)(2,1)S(1)} collective-permute-done((bf16[256,768]{1,0:T(8,128)(2,1)S(1)}, bf16[256,768]{1,0:T(8,128)(2,1)S(1)}, u32[]{:S(2)}, u32[]{:S(2)}) %collective-permute-start.16) | collective-permute-done | bytes 393248 | tf_op jit(solution)/shard_map/ppermute | solution.py:141
  73.0 1.6 %collective-permute-done.7 = bf16[256,256]{1,0:T(8,128)(2,1)S(1)} collective-permute-done((bf16[256,256]{1,0:T(8,128)(2,1)S(1)}, bf16[256,256]{1,0:T(8,128)(2,1)S(1)}, u32[]{:S(2)}, u32[]{:S(2)}) %collective-permute-start.7) | collective-permute-done | bytes 131104 | tf_op jit(solution)/shard_map/ppermute | solution.py:141
  74.6 5.6 %collective-permute-done.5 = bf16[256,512]{1,0:T(8,128)(2,1)S(1)} collective-permute-done((bf16[256,512]{1,0:T(8,128)(2,1)S(1)}, bf16[256,512]{1,0:T(8,128)(2,1)S(1)}, u32[]{:S(2)}, u32[]{:S(2)}) %collective-permute-start.5) | collective-permute-done | bytes 262176 | tf_op jit(solution)/shard_map/ppermute | solution.py:141
  81.3 1.4 %collective-permute-start.12 = (bf16[256,512]{1,0:T(8,128)(2,1)S(1)}, bf16[256,512]{1,0:T(8,128)(2,1)S(1)}, u32[]{:S(2)}, u32[]{:S(2)}) collective-permute-start(bf16[256,512]{1,0:T(8,128)(2,1)S(1)} %broadcast_select_fusion.3.refs_0_), channel_id=1, source_target_pairs={{0,24},{8,16},{16,8},{24,0},{1,25},{9,17},{17,9},{25,1},{2,26},{10... | collective-permute-start | bytes 786440 | tf_op jit(solution)/shard_map/ppermute | solution.py:133
  82.7 12.1 %collective-permute-done.18.refs_2_ = bf16[256,768]{1,0:T(8,128)(2,1)S(1)} collective-permute-done((bf16[256,768]{1,0:T(8,128)(2,1)S(1)}, bf16[256,768]{1,0:T(8,128)(2,1)S(1)}, u32[]{:S(2)}, u32[]{:S(2)}) %collective-permute-start.18) | collective-permute-done | bytes 393248 | tf_op jit(solution)/shard_map/ppermute | solution.py:133
  97.7 2.2 %copy-done.2 = bf16[2,1024,1024]{2,1,0:T(8,128)(2,1)S(1)} copy-done((bf16[2,1024,1024]{2,1,0:T(8,128)(2,1)S(1)}, bf16[2,1024,1024]{2,1,0:T(8,128)(2,1)}, u32[]{:S(2)}) %copy-start.2) | copy-done | bytes 4194328
  101.0 4.6 %last.1 = (f32[512,768]{1,0:T(8,128)S(1)}, bf16[256,768]{1,0:T(8,128)(2,1)S(1)}) custom-call(s32[3]{0:T(128)S(1)} %pad_add_fusion.where, bf16[256,768]{1,0:T(8,128)(2,1)S(1)} %broadcast_select_fusion.1.refs_0_, bf16[256,768]{1,0:T(8,128)(2,1)S(1)} %collective-permute-done.17.refs_1_, bf16[256,768]{1,0:T(8,128)(2,1)S(1)} %collective-permute-done.18.refs_2_, ...), custom_call_target="tpu_custom_call" | custom-call | flops 2415919104 | bytes 6039797 | tf_op jit(solution)/shard_map/last/pallas_call | solution.py:198
  105.6 3.5 %collective-permute-done.11.refs_5_ = bf16[256,256]{1,0:T(8,128)(2,1)S(1)} collective-permute-done((bf16[256,256]{1,0:T(8,128)(2,1)S(1)}, bf16[256,256]{1,0:T(8,128)(2,1)S(1)}, u32[]{:S(2)}, u32[]{:S(2)}) %collective-permute-start.11) | collective-permute-done | bytes 131104 | tf_op jit(solution)/shard_map/ppermute | solution.py:133
  109.2 5.5 %final.1 = bf16[512,768]{1,0:T(8,128)(2,1)} custom-call(s32[3]{0:T(128)S(1)} %pad_add_fusion.where, bf16[256,512]{1,0:T(8,128)(2,1)S(1)} %broadcast_select_fusion.3.refs_0_, bf16[256,256]{1,0:T(8,128)(2,1)S(1)} %broadcast_select_fusion.5.refs_1_, bf16[256,512]{1,0:T(8,128)(2,1)S(1)} %collective-permute-done.8.refs_2_, ...), custom_call_target="tpu_custom_call" | custom-call | flops 2415919104 | bytes 6039797 | tf_op jit(solution)/shard_map/final/pallas_call | solution.py:209
  (44 shorter events, 11.7 us)
Async XLA Ops:
  2.5 18.3 %copy-start.3 = (bf16[8,1,64,768]{3,2,1,0:T(8,128)(2,1)S(1)}, bf16[8,1,64,768]{3,2,1,0:T(8,128)(2,1)}, u32[]{:S(2)}) copy-start(bf16[8,1,64,768]{3,2,1,0:T(8,128)(2,1)} %param.4) | copy-start | bytes 2359300
  19.3 22.1 %collective-permute-start.3 = (bf16[4,256,256]{2,1,0:T(8,128)(2,1)S(1)}, bf16[4,256,256]{2,1,0:T(8,128)(2,1)}, u32[]{:S(2)}, u32[]{:S(2)}) collective-permute-start(bf16[4,256,256]{2,1,0:T(8,128)(2,1)S(1)} %all_to_all.10.refs_5_), channel_id=1, source_target_pairs={{0,1},{1,0},{2,3},{3,2},{4,5},{5,4},{6,7},{7,6},{8,9},{9,8},{10,11... | collective-permute-start | bytes 1572872 | tf_op jit(solution)/shard_map/ppermute | solution.py:153
  20.8 11.8 %collective-permute-start.2 = (bf16[256,768]{1,0:T(8,128)(2,1)S(1)}, bf16[256,768]{1,0:T(8,128)(2,1)}, u32[]{:S(2)}, u32[]{:S(2)}) collective-permute-start(bf16[256,768]{1,0:T(8,128)(2,1)S(1)} %bitcast.21), channel_id=1, source_target_pairs={{0,24},{8,16},{16,8},{24,0},{1,25},{9,17},{17,9},{25,1},{2,26},{10... | collective-permute-start | bytes 1179656 | tf_op jit(solution)/shard_map/ppermute | solution.py:133
  22.1 19.3 %collective-permute-start.1 = (bf16[256,768]{1,0:T(8,128)(2,1)S(1)}, bf16[256,768]{1,0:T(8,128)(2,1)}, u32[]{:S(2)}, u32[]{:S(2)}) collective-permute-start(bf16[256,768]{1,0:T(8,128)(2,1)S(1)} %bitcast.22), channel_id=1, source_target_pairs={{0,16},{8,24},{16,0},{24,8},{1,17},{9,25},{17,1},{25,9},{2,18},{10... | collective-permute-start | bytes 1179656 | tf_op jit(solution)/shard_map/ppermute | solution.py:133
  23.3 18.1 %collective-permute-start = (bf16[256,768]{1,0:T(8,128)(2,1)S(1)}, bf16[256,768]{1,0:T(8,128)(2,1)}, u32[]{:S(2)}, u32[]{:S(2)}) collective-permute-start(bf16[256,768]{1,0:T(8,128)(2,1)S(1)} %bitcast.23), channel_id=1, source_target_pairs={{0,8},{8,0},{16,24},{24,16},{1,9},{9,1},{17,25},{25,17},{2,10},{10... | collective-permute-start | bytes 1179656 | tf_op jit(solution)/shard_map/ppermute | solution.py:133
  23.6 34.5 %all-to-all-start.1 = ((bf16[4,256,256]{2,1,0:T(8,128)(2,1)}), bf16[4,256,256]{2,1,0:T(8,128)(2,1)}, u32[]{:S(2)}, u32[]{:S(2)}) async-start(bf16[4,256,256]{2,1,0:T(8,128)(2,1)} %get-tuple-element.9), calls=%async_computation.1 | async-start | bytes 1048576 | tf_op jit(solution)/shard_map/all_to_all | solution.py:150
  30.1 23.6 %collective-permute-start.15 = (bf16[256,768]{1,0:T(8,128)(2,1)S(1)}, bf16[256,768]{1,0:T(8,128)(2,1)}, u32[]{:S(2)}, u32[]{:S(2)}) collective-permute-start(bf16[256,768]{1,0:T(8,128)(2,1)S(1)} %bitcast.24), channel_id=1, source_target_pairs={{6,2},{7,3},{14,10},{15,11},{22,18},{23,19},{30,26},{31,27}} | collective-permute-start | bytes 1179656 | tf_op jit(solution)/shard_map/ppermute | solution.py:141
  41.4 2.2 %copy-start.1 = (bf16[2,1024,1024]{2,1,0:T(8,128)(2,1)S(1)}, bf16[2,1024,1024]{2,1,0:T(8,128)(2,1)}, u32[]{:S(2)}) copy-start(bf16[2,1024,1024]{2,1,0:T(8,128)(2,1)} %refs_8_.1) | copy-start | bytes 12582916
  46.6 12.5 %collective-permute-start.6 = (bf16[256,256]{1,0:T(8,128)(2,1)S(1)}, bf16[256,256]{1,0:T(8,128)(2,1)}, u32[]{:S(2)}, u32[]{:S(2)}) collective-permute-start(bf16[256,256]{1,0:T(8,128)(2,1)S(1)} %shard_map.38), channel_id=1, source_target_pairs={{6,2},{7,3},{14,10},{15,11},{22,18},{23,19},{30,26},{31,27}} | collective-permute-start | bytes 393224 | tf_op jit(solution)/shard_map/ppermute | solution.py:141
  52.3 6.9 %collective-permute-start.4 = (bf16[256,512]{1,0:T(8,128)(2,1)}, bf16[256,512]{1,0:T(8,128)(2,1)}, u32[]{:S(2)}, u32[]{:S(2)}) collective-permute-start(bf16[256,512]{1,0:T(8,128)(2,1)} %shard_map.37), channel_id=1, source_target_pairs={{6,2},{7,3},{14,10},{15,11},{22,18},{23,19},{30,26},{31,27}} | collective-permute-start | bytes 786440 | tf_op jit(solution)/shard_map/ppermute | solution.py:141
  53.8 18.0 %collective-permute-start.16 = (bf16[256,768]{1,0:T(8,128)(2,1)S(1)}, bf16[256,768]{1,0:T(8,128)(2,1)S(1)}, u32[]{:S(2)}, u32[]{:S(2)}) collective-permute-start(bf16[256,768]{1,0:T(8,128)(2,1)S(1)} %broadcast_select_fusion), channel_id=1, source_target_pairs={{2,0},{6,4},{0,2},{4,6},{3,1},{7,5},{1,3},{5,7},{10,8},{14,12},{8,... | collective-permute-start | bytes 1179656 | tf_op jit(solution)/shard_map/ppermute | solution.py:141
  58.1 38.2 %collective-permute-start.14 = (bf16[4,256,256]{2,1,0:T(8,128)(2,1)}, bf16[4,256,256]{2,1,0:T(8,128)(2,1)S(1)}, u32[]{:S(2)}, u32[]{:S(2)}) collective-permute-start(bf16[4,256,256]{2,1,0:T(8,128)(2,1)} %all-to-all-done.1.refs_9_), channel_id=1, source_target_pairs={{0,1},{1,0},{2,3},{3,2},{4,5},{5,4},{6,7},{7,6},{8,9},{9,8},{10,11... | collective-permute-start | bytes 1572872 | tf_op jit(solution)/shard_map/ppermute | solution.py:153
  59.1 15.5 %collective-permute-start.7 = (bf16[256,256]{1,0:T(8,128)(2,1)S(1)}, bf16[256,256]{1,0:T(8,128)(2,1)S(1)}, u32[]{:S(2)}, u32[]{:S(2)}) collective-permute-start(bf16[256,256]{1,0:T(8,128)(2,1)S(1)} %broadcast_select_fusion.4), channel_id=1, source_target_pairs={{2,0},{6,4},{0,2},{4,6},{3,1},{7,5},{1,3},{5,7},{10,8},{14,12},{8,... | collective-permute-start | bytes 393224 | tf_op jit(solution)/shard_map/ppermute | solution.py:141
  60.2 20.0 %collective-permute-start.5 = (bf16[256,512]{1,0:T(8,128)(2,1)S(1)}, bf16[256,512]{1,0:T(8,128)(2,1)S(1)}, u32[]{:S(2)}, u32[]{:S(2)}) collective-permute-start(bf16[256,512]{1,0:T(8,128)(2,1)S(1)} %broadcast_select_fusion.2), channel_id=1, source_target_pairs={{2,0},{6,4},{0,2},{4,6},{3,1},{7,5},{1,3},{5,7},{10,8},{14,12},{8,... | collective-permute-start | bytes 786440 | tf_op jit(solution)/shard_map/ppermute | solution.py:141
  71.8 9.5 %collective-permute-start.19 = (bf16[256,768]{1,0:T(8,128)(2,1)S(1)}, bf16[256,768]{1,0:T(8,128)(2,1)S(1)}, u32[]{:S(2)}, u32[]{:S(2)}) collective-permute-start(bf16[256,768]{1,0:T(8,128)(2,1)S(1)} %broadcast_select_fusion.1.refs_0_), channel_id=1, source_target_pairs={{0,24},{8,16},{16,8},{24,0},{1,25},{9,17},{17,9},{25,1},{2,26},{10... | collective-permute-start | bytes 1179656 | tf_op jit(solution)/shard_map/ppermute | solution.py:133
  73.0 21.8 %collective-permute-start.18 = (bf16[256,768]{1,0:T(8,128)(2,1)S(1)}, bf16[256,768]{1,0:T(8,128)(2,1)S(1)}, u32[]{:S(2)}, u32[]{:S(2)}) collective-permute-start(bf16[256,768]{1,0:T(8,128)(2,1)S(1)} %broadcast_select_fusion.1.refs_0_), channel_id=1, source_target_pairs={{0,16},{8,24},{16,0},{24,8},{1,17},{9,25},{17,1},{25,9},{2,18},{10... | collective-permute-start | bytes 1179656 | tf_op jit(solution)/shard_map/ppermute | solution.py:133
  74.6 20.5 %collective-permute-start.17 = (bf16[256,768]{1,0:T(8,128)(2,1)S(1)}, bf16[256,768]{1,0:T(8,128)(2,1)S(1)}, u32[]{:S(2)}, u32[]{:S(2)}) collective-permute-start(bf16[256,768]{1,0:T(8,128)(2,1)S(1)} %broadcast_select_fusion.1.refs_0_), channel_id=1, source_target_pairs={{0,8},{8,0},{16,24},{24,16},{1,9},{9,1},{17,25},{25,17},{2,10},{10... | collective-permute-start | bytes 1179656 | tf_op jit(solution)/shard_map/ppermute | solution.py:133
  80.2 16.5 %collective-permute-start.13 = (bf16[256,256]{1,0:T(8,128)(2,1)S(1)}, bf16[256,256]{1,0:T(8,128)(2,1)S(1)}, u32[]{:S(2)}, u32[]{:S(2)}) collective-permute-start(bf16[256,256]{1,0:T(8,128)(2,1)S(1)} %broadcast_select_fusion.5.refs_1_), channel_id=1, source_target_pairs={{0,24},{8,16},{16,8},{24,0},{1,25},{9,17},{17,9},{25,1},{2,26},{10... | collective-permute-start | bytes 393224 | tf_op jit(solution)/shard_map/ppermute | solution.py:133
  81.3 27.8 %collective-permute-start.12 = (bf16[256,512]{1,0:T(8,128)(2,1)S(1)}, bf16[256,512]{1,0:T(8,128)(2,1)S(1)}, u32[]{:S(2)}, u32[]{:S(2)}) collective-permute-start(bf16[256,512]{1,0:T(8,128)(2,1)S(1)} %broadcast_select_fusion.3.refs_0_), channel_id=1, source_target_pairs={{0,24},{8,16},{16,8},{24,0},{1,25},{9,17},{17,9},{25,1},{2,26},{10... | collective-permute-start | bytes 786440 | tf_op jit(solution)/shard_map/ppermute | solution.py:133
  94.8 14.4 %collective-permute-start.10 = (bf16[256,512]{1,0:T(8,128)(2,1)S(1)}, bf16[256,512]{1,0:T(8,128)(2,1)S(1)}, u32[]{:S(2)}, u32[]{:S(2)}) collective-permute-start(bf16[256,512]{1,0:T(8,128)(2,1)S(1)} %broadcast_select_fusion.3.refs_0_), channel_id=1, source_target_pairs={{0,16},{8,24},{16,0},{24,8},{1,17},{9,25},{17,1},{25,9},{2,18},{10... | collective-permute-start | bytes 786440 | tf_op jit(solution)/shard_map/ppermute | solution.py:133
  95.1 14.1 %collective-permute-start.8 = (bf16[256,512]{1,0:T(8,128)(2,1)S(1)}, bf16[256,512]{1,0:T(8,128)(2,1)S(1)}, u32[]{:S(2)}, u32[]{:S(2)}) collective-permute-start(bf16[256,512]{1,0:T(8,128)(2,1)S(1)} %broadcast_select_fusion.3.refs_0_), channel_id=1, source_target_pairs={{0,8},{8,0},{16,24},{24,16},{1,9},{9,1},{17,25},{25,17},{2,10},{10... | collective-permute-start | bytes 786440 | tf_op jit(solution)/shard_map/ppermute | solution.py:133
  96.3 12.8 %collective-permute-start.11 = (bf16[256,256]{1,0:T(8,128)(2,1)S(1)}, bf16[256,256]{1,0:T(8,128)(2,1)S(1)}, u32[]{:S(2)}, u32[]{:S(2)}) collective-permute-start(bf16[256,256]{1,0:T(8,128)(2,1)S(1)} %broadcast_select_fusion.5.refs_1_), channel_id=1, source_target_pairs={{0,16},{8,24},{16,0},{24,8},{1,17},{9,25},{17,1},{25,9},{2,18},{10... | collective-permute-start | bytes 393224 | tf_op jit(solution)/shard_map/ppermute | solution.py:133
  96.8 12.4 %collective-permute-start.9 = (bf16[256,256]{1,0:T(8,128)(2,1)S(1)}, bf16[256,256]{1,0:T(8,128)(2,1)S(1)}, u32[]{:S(2)}, u32[]{:S(2)}) collective-permute-start(bf16[256,256]{1,0:T(8,128)(2,1)S(1)} %broadcast_select_fusion.5.refs_1_), channel_id=1, source_target_pairs={{0,8},{8,0},{16,24},{24,16},{1,9},{9,1},{17,25},{25,17},{2,10},{10... | collective-permute-start | bytes 393224 | tf_op jit(solution)/shard_map/ppermute | solution.py:133
  97.7 2.2 %copy-start.2 = (bf16[2,1024,1024]{2,1,0:T(8,128)(2,1)S(1)}, bf16[2,1024,1024]{2,1,0:T(8,128)(2,1)}, u32[]{:S(2)}) copy-start(bf16[2,1024,1024]{2,1,0:T(8,128)(2,1)} %refs_8_.1) | copy-start | bytes 12582916
  (2 other events, 2.7 us)
where the time goes:
time: 115 us
  waiting for transfers between devices  40.7 us (35%)
  starting transfers between devices  30.2 us (26%)
  Pallas kernels  17.5 us (15%)
  blocking collectives  16 us (14%)
  local copies, waits for them, and re-layouts  8.88 us (8%)
  other arithmetic  1.25 us (1%)
    ppermute x12, waiting for transfers between devices, gather_rows(): lax.ppermute(value, 'row', pairs[d])  25.5 us
    all_to_all x1, blocking collectives, spread_coeffs(): return lax.all_to_all(halves[which], 'col', 0, 0, tiled=True)  16 us
    ppermute x6, waiting for transfers between devices, step_down(): got = lax.ppermute(value, 'col', pairs)  15.2 us
    ppermute x6, starting transfers between devices, step_down(): got = lax.ppermute(value, 'col', pairs)  12 us
    ppermute x12, starting transfers between devices, gather_rows(): lax.ppermute(value, 'row', pairs[d])  9.19 us
    pallas_call x2, Pallas kernels, local(): pl.pallas_call(functools.partial(mid_kernel, row_count, rows, (per_col -...  7.41 us
    unnamed x11, local copies, waits for them, and re-layouts  7.25 us
    all_to_all x1, starting transfers between devices, spread_coeffs(): return lax.all_to_all(halves[which], 'col', 0, 0, tiled=True)  6.54 us
  transfers between devices with their start and end apart: 21, of which 7 were waited for; matrix products, arithmetic and copies ran while one was open for 1% of the time, Pallas kernels for 10%

commit v1 on v0

v1 whole, which is shorter than its diff:
```python
import functools

import jax
import jax.numpy as jnp
from jax import lax
from jax.experimental import pallas as pl
from jax.experimental.pallas import tpu as pltpu
from jax.sharding import PartitionSpec as P

BOTH = True
STEP = 256
VMEM = pl.BlockSpec(memory_space=pltpu.VMEM)
SMEM = pl.BlockSpec(memory_space=pltpu.SMEM)


def chunk_bounds(voxels):
    cut = voxels // 256 * 2 // 3 * 256 or voxels // 2
    return [slice(0, cut), slice(cut, voxels)]


def dot(a, b):
    return jnp.dot(a, b, preferred_element_type=jnp.float32)


def assemble(full, pieces, row_pos, rows):
    count = len(pieces)
    tail = pieces[0].shape[0] // rows
    for d, piece in enumerate(pieces):
        p = row_pos ^ d
        for k in range(tail):
            at = pl.multiple_of((k * count + p) * rows, rows)
            full[pl.ds(at, rows), :] = piece[k * rows : (k + 1) * rows, :]


def solve_step(x, inverse, full):
    step = inverse.shape[1]
    at = pl.multiple_of(pl.program_id(0) * step, step)
    x[pl.ds(at, step), :] = dot(inverse[0], full[...]).astype(x.dtype)


def first_step(f):
    pl.when(pl.program_id(0) == 0)(f)


def last_step(f):
    pl.when(pl.program_id(0) == pl.num_programs(0) - 1)(f)


def subtract(total, coeffs, x, at=slice(None)):
    own = coeffs.shape[2]
    for c in range(coeffs.shape[0]):
        total = total - dot(coeffs[c, at, :], x[c * own : (c + 1) * own, :])
    return total


def own_rows(x, row_pos, count, rows):
    tail = x.shape[0] // (count * rows)
    return [x[pl.ds(pl.multiple_of((k * count + row_pos) * rows, rows), rows), :] for k in range(tail)]


def mid_kernel(row_count, rows, start, cols, where, *refs):
    pieces = [ref.at[:, cols] for ref in refs[:row_count]]
    inverse, *halves, mid, out, full, x = refs[row_count:]
    half, piece = halves[0].shape[1], mid.shape[0]

    @pl.when(where[2] == 1)
    def _():
        first_step(lambda: assemble(full, pieces, where[0], rows))
        solve_step(x, inverse, full)

        @last_step
        def _():
            for h in range(2):
                low, high = max(start, h * half), min(start + piece, (h + 1) * half)
                if low >= high:
                    continue
                to = slice(low - start, high - start)

                def rest(coeffs):
                    total = mid[to, cols].astype(jnp.float32)
                    total = subtract(total, coeffs, x, slice(low - h * half, high - h * half))
                    out[to, :] = total.astype(out.dtype)

                if len(halves) == 1:
                    rest(halves[0])
                else:
                    pl.when(where[1] == h)(functools.partial(rest, halves[0]))
                    pl.when(where[1] != h)(functools.partial(rest, halves[1]))

    @pl.when(where[2] == 0)
    def _():
        out[...] = jnp.zeros_like(out)


def last_kernel(row_count, rows, where, *refs):
    pieces = refs[:row_count]
    inverse, mine, other, rhs, acc, x_rows, full, x = refs[row_count:]
    first_step(lambda: assemble(full, pieces, where[0], rows))
    solve_step(x, inverse, full)

    @last_step
    def _():
        for k, part in enumerate(own_rows(x, where[0], row_count, rows)):
            x_rows[k * rows : (k + 1) * rows, :] = part
        half = mine.shape[1]
        for coeffs, h in ((mine, where[1]), (other, 1 - where[1])):
            at = pl.multiple_of(h * half, half)
            acc[pl.ds(at, half), :] = subtract(rhs[pl.ds(at, half), :].astype(jnp.float32), coeffs, x)


def final_kernel(row_count, rows, cols, where, *refs):
    pieces = refs[:row_count]
    inverse, mine, other, acc, x_rows, *_, out, full, x = refs[row_count:]
    first_step(lambda: assemble(full, pieces, where[0], rows))
    solve_step(x, inverse, full)

    @last_step
    def _():
        half = mine.shape[1]
        for coeffs, h in ((mine, where[1]), (other, 1 - where[1])):
            at = pl.multiple_of(h * half, half)
            out[pl.ds(at, half), :] = subtract(acc[pl.ds(at, half), cols], coeffs, x).astype(out.dtype)

        @pl.when(where[2] == 1)
        def _():
            piece = x_rows.shape[0]
            start = out.shape[0] - 2 * piece
            for k, part in enumerate(own_rows(x, where[0], row_count, rows)):
                out[start + k * rows : start + (k + 1) * rows, :] = part
            out[start + piece :, :] = x_rows[:, cols]


def local(coeffs_r, rhs, inverses):
    row_count = lax.axis_size("row")
    col_count = lax.axis_size("col")
    vox_count = lax.axis_size("vox")
    row_pos = lax.axis_index("row")
    col_pos = lax.axis_index("col")
    vox_pos = lax.axis_index("vox")
    per_col = rhs.shape[0]
    rows = rhs.shape[2]
    voxels = rhs.shape[3]
    own = coeffs_r.shape[4]
    order = inverses.shape[1]
    tail = order // (rows * row_count)
    piece = tail * rows
    owner = col_count - 1
    where = jnp.stack([row_pos, vox_pos, (col_pos == owner).astype(jnp.int32)]).astype(jnp.int32)
    bf16 = jnp.bfloat16

    def gather_rows(value):
        pairs = [[(r, r ^ d) for r in range(row_count)] for d in range(row_count)]
        return [value] + [lax.ppermute(value, "row", pairs[d]) for d in range(1, row_count)]

    def take(value, got, targets):
        is_target = functools.reduce(jnp.logical_or, [col_pos == t for t in targets])
        return jnp.where(is_target, got, value)

    def step_down(value, step, both_ways=False):
        stride = col_count >> (step + 1)
        targets = list(range(stride - 1, owner, 2 * stride))
        if both_ways and len(targets) > 1:
            high = targets.pop()
            got = lax.ppermute(value, "col", [(high - stride, high)])
            lower = lax.ppermute(value, "col", [(t + stride, t) for t in targets])
            return take(take(value, lower, targets), got, [high])
        pairs = [(t + stride, t) for t in targets]
        if stride == 1:
            pairs += [(t, t + stride) for t in targets]
        return take(value, lax.ppermute(value, "col", pairs), targets)

    half = per_col // vox_count
    split = coeffs_r.reshape(col_count, vox_count, half * rows, 2, own)
    direct = per_col == 2 * tail
    mine = lax.dynamic_slice_in_dim(split, vox_pos, 1, 1)
    if direct:
        mine = jnp.concatenate([mine[:owner], split[owner:, :1]], 0)
    halves = mine[:, 0].transpose(2, 0, 1, 3)

    def spread_coeffs(which):
        return lax.all_to_all(halves[which], "col", 0, 0, tiled=True)

    def swap(value):
        return lax.ppermute(value, "vox", [(0, 1), (1, 0)])

    step = min(STEP, order)

    def call(body, args, specs, out_shape, out_specs, which, width, n_rows, aliases=None):
        flops = 2 * order * width * (order + n_rows)
        return pl.pallas_call(
            body,
            grid=(order // step,),
            out_shape=out_shape,
            in_specs=[SMEM] + [VMEM] * row_count + [pl.BlockSpec((1, step, order), lambda m: (which, m, 0))] + specs,
            out_specs=out_specs,
            scratch_shapes=[pltpu.VMEM((order, width), bf16), pltpu.VMEM((order, width), bf16)],
            input_output_aliases=aliases or {},
            compiler_params=pltpu.CompilerParams(vmem_limit_bytes=16 << 20),
            cost_estimate=pl.CostEstimate(flops=flops, bytes_accessed=flops // 400, transcendentals=0),
        )(where, *args)

    downs = col_count.bit_length() - 1
    bounds = chunk_bounds(voxels)
    mid_piece = rhs[per_col - 2 * tail : per_col - tail].reshape(piece, voxels)
    last_piece = rhs[per_col - tail :].reshape(piece, voxels)

    top = gather_rows(last_piece)
    spread = step_down(last_piece, 0)
    mine_1 = spread_coeffs(1)
    for s in range(1, downs):
        spread = step_down(spread, s, both_ways=BOTH)
    other_1 = swap(mine_1)
    panels = [mine_1] if direct else [mine_1, other_1]

    mids = []
    for cols in bounds:
        width = cols.stop - cols.start
        body = functools.partial(mid_kernel, row_count, rows, (per_col - 2 * tail) * rows, cols)
        shape = jax.ShapeDtypeStruct((piece, width), bf16)
        args = (*top, pltpu.with_memory_space_constraint(inverses, pltpu.HBM), *panels, mid_piece)
        mids.append(call(body, args, [VMEM] * (len(panels) + 1), shape, VMEM, 1, width, piece))
    mids = [step_down(mid, 0) for mid in mids]
    last = gather_rows(spread)
    for s in range(1, downs):
        mids = [step_down(mid, s) for mid in mids]
    mine_0 = spread_coeffs(0)
    middle = [gather_rows(mid) for mid in mids]
    other_0 = swap(mine_0)

    flat = rhs.reshape(per_col * rows, voxels)
    acc, x_rows = call(
        functools.partial(last_kernel, row_count, rows),
        (*last, inverses, mine_1, other_1, flat),
        [VMEM] * 3,
        (jax.ShapeDtypeStruct(flat.shape, jnp.float32), jax.ShapeDtypeStruct((piece, voxels), bf16)),
        (VMEM, VMEM),
        1,
        voxels,
        per_col * rows,
    )
    out = None
    for n, cols in enumerate(bounds):
        width = cols.stop - cols.start
        block = cols.start // width
        done = [] if out is None else [out]
        out = call(
            functools.partial(final_kernel, row_count, rows, cols),
            (*middle[n], inverses, mine_0, other_0, acc, x_rows, *done),
            [VMEM] * 4 + [pl.BlockSpec(memory_space=pl.ANY)] * len(done),
            jax.ShapeDtypeStruct(flat.shape, bf16),
            pl.BlockSpec((per_col * rows, width), functools.partial(lambda block, m: (0, block), block)),
            0,
            width,
            per_col * rows,
            {row_count + 6: 0} if done else None,
        )
    return out.reshape(rhs.shape)


def solution(mesh):
    placed = (P(None, "row", None, None, "col"), P("col", "row", None, "vox"), P())

    return jax.shard_map(local, mesh=mesh, in_specs=placed, out_specs=P("col", "row", None, "vox"), check_vma=False)
```

time: 115 us -> 102 us (0.89)
  the two profiles are of different devices: /device:TPU:21 before, /device:TPU:0 now
where the time goes in v1:
time: 102 us; the launch traced here: 101 us
  starting transfers between devices  43.5 us (43%)
  waiting for transfers between devices  32.3 us (32%)
  Pallas kernels  16.4 us (16%)
  local copies, waits for them, and re-layouts  6.27 us (6%)
  other arithmetic  2.26 us (2%)
    all_to_all x2, waiting for transfers between devices, spread_coeffs(): return lax.all_to_all(halves[which], 'col', 0, 0, tiled=True)  18.5 us
    pallas_call x5, Pallas kernels, call(): pl.pallas_call(body, grid=(order // step,), out_shape=out_shape, in_specs...  16.4 us
    ppermute x5, starting transfers between devices, step_down(): return take(value, lax.ppermute(value, 'col', pairs), targets)  16.1 us
    ppermute x12, starting transfers between devices, gather_rows(): lax.ppermute(value, 'row', pairs[d])  15.5 us
    ppermute x12, waiting for transfers between devices, gather_rows(): lax.ppermute(value, 'row', pairs[d])  10.4 us
    all_to_all x2, starting transfers between devices, spread_coeffs(): return lax.all_to_all(halves[which], 'col', 0, 0, tiled=True)  9.82 us
    ppermute x5, waiting for transfers between devices, step_down(): return take(value, lax.ppermute(value, 'col', pairs), targets)  3.21 us
    slice x2, local copies, waits for them, and re-layouts, local(): mine = jnp.concatenate([mine[:owner], split[owner:, :1]], 0)  2.82 us
  transfers between devices with their start and end apart: 23, of which 6 were waited for; matrix products, arithmetic and copies ran while one was open for 2% of the time, Pallas kernels for 13%

profile of v1, /device:TPU:0, one launch (start us, length us, event | category | flops | bytes accessed | tf_op | source)
XLA Modules:
  0.0 101.0 jit_solution(449862757700516378)
XLA Ops:
  0.0 1.1 %slice.24 = bf16[1,1,256,2,256]{4,3,2,1,0:T(2,128)(2,1)S(1)} slice(bf16[4,2,256,2,256]{4,3,2,1,0:T(2,128)(2,1)} %bitcast.28), slice={[3:4], [0:1], [0:256], [0:2], [0:256]} | slice | bytes 524288 | tf_op jit(solution)/shard_map/slice | solution.py:177
  1.2 1.7 %constant_dynamic-slice_fusion = bf16[3,1,256,2,256]{4,3,2,1,0:T(2,128)(2,1)S(1)} fusion(bf16[4,2,256,2,256]{4,3,2,1,0:T(2,128)(2,1)} %bitcast.29, s32[]{:T(128)S(6)} %select_n.53), kind=kLoop, calls=%fused_computation.10 | loop fusion | bytes 1572868 | tf_op jit(solution)/shard_map/slice | solution.py:177
  3.1 1.1 %slice_bitcast_fusion = (bf16[4,256,256]{2,1,0:T(8,128)(2,1)}, bf16[4,256,256]{2,1,0:T(8,128)(2,1)}) fusion(bf16[2,4,256,256]{3,2,1,0:T(8,128)(2,1)S(1)} %maximum_bitcast_fusion), kind=kLoop, calls=%fused_computation.1 | loop fusion | bytes 2097152 | tf_op jit(solution)/shard_map/squeeze | solution.py:181
  4.2 6.3 %all-to-all-start = ((bf16[4,256,256]{2,1,0:T(8,128)(2,1)}), bf16[4,256,256]{2,1,0:T(8,128)(2,1)S(1)}, u32[]{:S(2)}, u32[]{:S(2)}) async-start(bf16[4,256,256]{2,1,0:T(8,128)(2,1)} %get-tuple-element.10), calls=%async_computation | async-start | bytes 1048576 | tf_op jit(solution)/shard_map/all_to_all | solution.py:181
  10.6 2.5 %collective-permute-start.2 = (bf16[256,768]{1,0:T(8,128)(2,1)S(1)}, bf16[256,768]{1,0:T(8,128)(2,1)S(1)}, u32[]{:S(2)}, u32[]{:S(2)}) collective-permute-start(bf16[256,768]{1,0:T(8,128)(2,1)S(1)} %bitcast.19), channel_id=1, source_target_pairs={{0,24},{8,16},{16,8},{24,0},{1,25},{9,17},{17,9},{25,1},{2,26},{10... | collective-permute-start | bytes 1179656 | tf_op jit(solution)/shard_map/ppermute | solution.py:153
  14.9 18.5 %all-to-all-done.refs_5_ = bf16[4,256,256]{2,1,0:T(8,128)(2,1)S(1)} async-done(((bf16[4,256,256]{2,1,0:T(8,128)(2,1)}), bf16[4,256,256]{2,1,0:T(8,128)(2,1)S(1)}, u32[]{:S(2)}, u32[]{:S(2)}) %all-to-all-start) | async-done | bytes 524320 | tf_op jit(solution)/shard_map/all_to_all | solution.py:181
  33.4 3.5 %all-to-all-start.1 = ((bf16[4,256,256]{2,1,0:T(8,128)(2,1)}), bf16[4,256,256]{2,1,0:T(8,128)(2,1)S(1)}, u32[]{:S(2)}, u32[]{:S(2)}) async-start(bf16[4,256,256]{2,1,0:T(8,128)(2,1)} %get-tuple-element.9), calls=%async_computation.1 | async-start | bytes 1048576 | tf_op jit(solution)/shard_map/all_to_all | solution.py:181
  36.9 2.4 %shard_map.37 = bf16[256,256]{1,0:T(8,128)(2,1)S(1)} custom-call(s32[3]{0:T(128)S(1)} %pad_add_fusion.where, bf16[256,768]{1,0:T(8,128)(2,1)S(1)} %bitcast.23, bf16[256,768]{1,0:T(8,128)(2,1)S(1)} %collective-permute-done.refs_1_, bf16[256,768]{1,0:T(8,128)(2,1)S(1)} %collective-permute-done.1.refs_2_, bf16[256,768]{1,0:T(8,128)(2,1)S(1)} %collective-permute-done.2.refs_3_, ...), custom_call_target="tpu_custom_call" | custom-call | flops 671088640 | bytes 1677721 | tf_op jit(solution)/shard_map/pallas_call | solution.py:190
  40.0 2.4 %shard_map.39 = bf16[256,512]{1,0:T(8,128)(2,1)S(1)} custom-call(s32[3]{0:T(128)S(1)} %pad_add_fusion.where, bf16[256,768]{1,0:T(8,128)(2,1)S(1)} %bitcast.24, bf16[256,768]{1,0:T(8,128)(2,1)S(1)} %collective-permute-done.refs_1_, bf16[256,768]{1,0:T(8,128)(2,1)S(1)} %collective-permute-done.1.refs_2_, bf16[256,768]{1,0:T(8,128)(2,1)S(1)} %collective-permute-done.2.refs_3_, ...), custom_call_target="tpu_custom_call" | custom-call | flops 1342177280 | bytes 3355443 | tf_op jit(solution)/shard_map/pallas_call | solution.py:190
  43.2 1.4 %collective-permute-start.11 = (bf16[256,768]{1,0:T(8,128)(2,1)S(1)}, bf16[256,768]{1,0:T(8,128)(2,1)S(1)}, u32[]{:S(2)}, u32[]{:S(2)}) collective-permute-start(bf16[256,768]{1,0:T(8,128)(2,1)S(1)} %broadcast_select_fusion), channel_id=1, source_target_pairs={{2,0},{3,1},{10,8},{11,9},{18,16},{19,17},{26,24},{27,25}} | collective-permute-start | bytes 1179656 | tf_op jit(solution)/shard_map/ppermute | solution.py:165
  45.4 8.4 %collective-permute-start.4 = (bf16[256,256]{1,0:T(8,128)(2,1)S(1)}, bf16[256,256]{1,0:T(8,128)(2,1)}, u32[]{:S(2)}, u32[]{:S(2)}) collective-permute-start(bf16[256,256]{1,0:T(8,128)(2,1)S(1)} %broadcast_select_fusion.3), channel_id=1, source_target_pairs={{2,0},{6,4},{0,2},{4,6},{3,1},{7,5},{1,3},{5,7},{10,8},{14,12},{8,... | collective-permute-start | bytes 393224 | tf_op jit(solution)/shard_map/ppermute | solution.py:170
  53.8 5.6 %collective-permute-start.17 = (bf16[256,512]{1,0:T(8,128)(2,1)S(1)}, bf16[256,512]{1,0:T(8,128)(2,1)}, u32[]{:S(2)}, u32[]{:S(2)}) collective-permute-start(bf16[256,512]{1,0:T(8,128)(2,1)S(1)} %broadcast_select_fusion.1), channel_id=1, source_target_pairs={{2,0},{6,4},{0,2},{4,6},{3,1},{7,5},{1,3},{5,7},{10,8},{14,12},{8,... | collective-permute-start | bytes 786440 | tf_op jit(solution)/shard_map/ppermute | solution.py:170
  59.7 2.5 %collective-permute-start.14 = (bf16[256,768]{1,0:T(8,128)(2,1)S(1)}, bf16[256,768]{1,0:T(8,128)(2,1)S(1)}, u32[]{:S(2)}, u32[]{:S(2)}) collective-permute-start(bf16[256,768]{1,0:T(8,128)(2,1)S(1)} %select_select_fusion.refs_0_), channel_id=1, source_target_pairs={{0,24},{8,16},{16,8},{24,0},{1,25},{9,17},{17,9},{25,1},{2,26},{10... | collective-permute-start | bytes 1179656 | tf_op jit(solution)/shard_map/ppermute | solution.py:153
  63.2 3.2 %collective-permute-done.17 = bf16[256,512]{1,0:T(8,128)(2,1)} collective-permute-done((bf16[256,512]{1,0:T(8,128)(2,1)S(1)}, bf16[256,512]{1,0:T(8,128)(2,1)}, u32[]{:S(2)}, u32[]{:S(2)}) %collective-permute-start.17) | collective-permute-done | bytes 262176 | tf_op jit(solution)/shard_map/ppermute | solution.py:170
  67.4 5.2 %collective-permute-done.14.refs_3_ = bf16[256,768]{1,0:T(8,128)(2,1)S(1)} collective-permute-done((bf16[256,768]{1,0:T(8,128)(2,1)S(1)}, bf16[256,768]{1,0:T(8,128)(2,1)S(1)}, u32[]{:S(2)}, u32[]{:S(2)}) %collective-permute-start.14) | collective-permute-done | bytes 393248 | tf_op jit(solution)/shard_map/ppermute | solution.py:153
  72.6 2.4 %collective-permute-start.20 = (bf16[256,512]{1,0:T(8,128)(2,1)S(1)}, bf16[256,512]{1,0:T(8,128)(2,1)S(1)}, u32[]{:S(2)}, u32[]{:S(2)}) collective-permute-start(bf16[256,512]{1,0:T(8,128)(2,1)S(1)} %broadcast_select_fusion.2.refs_0_), channel_id=1, source_target_pairs={{0,24},{8,16},{16,8},{24,0},{1,25},{9,17},{17,9},{25,1},{2,26},{10... | collective-permute-start | bytes 786440 | tf_op jit(solution)/shard_map/ppermute | solution.py:153
  75.1 5.0 %collective-permute-done.13.refs_2_ = bf16[256,768]{1,0:T(8,128)(2,1)} collective-permute-done((bf16[256,768]{1,0:T(8,128)(2,1)S(1)}, bf16[256,768]{1,0:T(8,128)(2,1)}, u32[]{:S(2)}, u32[]{:S(2)}) %collective-permute-start.13) | collective-permute-done | bytes 393248 | tf_op jit(solution)/shard_map/ppermute | solution.py:153
  80.1 1.5 %collective-permute-start.19 = (bf16[256,512]{1,0:T(8,128)(2,1)S(1)}, bf16[256,512]{1,0:T(8,128)(2,1)S(1)}, u32[]{:S(2)}, u32[]{:S(2)}) collective-permute-start(bf16[256,512]{1,0:T(8,128)(2,1)S(1)} %broadcast_select_fusion.2.refs_0_), channel_id=1, source_target_pairs={{0,16},{8,24},{16,0},{24,8},{1,17},{9,25},{17,1},{25,9},{2,18},{10... | collective-permute-start | bytes 786440 | tf_op jit(solution)/shard_map/ppermute | solution.py:153
  83.3 1.2 %collective-permute-start.7 = (bf16[256,256]{1,0:T(8,128)(2,1)S(1)}, bf16[256,256]{1,0:T(8,128)(2,1)S(1)}, u32[]{:S(2)}, u32[]{:S(2)}) collective-permute-start(bf16[256,256]{1,0:T(8,128)(2,1)S(1)} %broadcast_select_fusion.4.refs_0_), channel_id=1, source_target_pairs={{0,24},{8,16},{16,8},{24,0},{1,25},{9,17},{17,9},{25,1},{2,26},{10... | collective-permute-start | bytes 393224 | tf_op jit(solution)/shard_map/ppermute | solution.py:153
  84.6 2.2 %copy-done = bf16[2,1024,1024]{2,1,0:T(8,128)(2,1)S(1)} copy-done((bf16[2,1024,1024]{2,1,0:T(8,128)(2,1)S(1)}, bf16[2,1024,1024]{2,1,0:T(8,128)(2,1)}, u32[]{:S(2)}) %copy-start) | copy-done | bytes 4194328
  86.8 4.6 %shard_map.38 = (f32[512,768]{1,0:T(8,128)S(1)}, bf16[256,768]{1,0:T(8,128)(2,1)S(1)}) custom-call(s32[3]{0:T(128)S(1)} %pad_add_fusion.where, bf16[256,768]{1,0:T(8,128)(2,1)S(1)} %select_select_fusion.refs_0_, bf16[256,768]{1,0:T(8,128)(2,1)} %collective-permute-done.12.refs_1_, bf16[256,768]{1,0:T(8,128)(2,1)} %collective-permute-done.13.refs_2_, ...), custom_call_target="tpu_custom_call" | custom-call | flops 2415919104 | bytes 6039797 | tf_op jit(solution)/shard_map/pallas_call | solution.py:190
  91.4 1.6 %collective-permute-start.6 = (bf16[256,256]{1,0:T(8,128)(2,1)S(1)}, bf16[256,256]{1,0:T(8,128)(2,1)S(1)}, u32[]{:S(2)}, u32[]{:S(2)}) collective-permute-start(bf16[256,256]{1,0:T(8,128)(2,1)S(1)} %broadcast_select_fusion.4.refs_0_), channel_id=1, source_target_pairs={{0,16},{8,24},{16,0},{24,8},{1,17},{9,25},{17,1},{25,9},{2,18},{10... | collective-permute-start | bytes 393224 | tf_op jit(solution)/shard_map/ppermute | solution.py:153
  93.8 4.0 %shard_map.40.refs_9_ = bf16[512,768]{1,0:T(8,128)(2,1)} custom-call(s32[3]{0:T(128)S(1)} %pad_add_fusion.where, bf16[256,512]{1,0:T(8,128)(2,1)S(1)} %broadcast_select_fusion.2.refs_0_, bf16[256,512]{1,0:T(8,128)(2,1)S(1)} %collective-permute-done.18.refs_1_, bf16[256,512]{1,0:T(8,128)(2,1)S(1)} %collective-permute-done.19.refs_2_, ...), custom_call_target="tpu_custom_call" | custom-call | flops 1610612736 | bytes 4026531 | tf_op jit(solution)/shard_map/pallas_call | solution.py:190
  98.0 3.0 %shard_map.41 = bf16[512,768]{1,0:T(8,128)(2,1)} custom-call(s32[3]{0:T(128)S(1)} %pad_add_fusion.where, bf16[256,256]{1,0:T(8,128)(2,1)S(1)} %broadcast_select_fusion.4.refs_0_, bf16[256,256]{1,0:T(8,128)(2,1)S(1)} %collective-permute-done.5.refs_1_, bf16[256,256]{1,0:T(8,128)(2,1)S(1)} %collective-permute-done.6.refs_2_, ...), custom_call_target="tpu_custom_call", output_to_operand_aliasing={{}: (10, {})} | custom-call | flops 805306368 | bytes 2013265 | tf_op jit(solution)/shard_map/pallas_call | solution.py:190
  (47 shorter events, 9.2 us)
Async XLA Ops:
  4.2 29.3 %all-to-all-start = ((bf16[4,256,256]{2,1,0:T(8,128)(2,1)}), bf16[4,256,256]{2,1,0:T(8,128)(2,1)S(1)}, u32[]{:S(2)}, u32[]{:S(2)}) async-start(bf16[4,256,256]{2,1,0:T(8,128)(2,1)} %get-tuple-element.10), calls=%async_computation | async-start | bytes 1048576 | tf_op jit(solution)/shard_map/all_to_all | solution.py:181
  10.6 26.3 %collective-permute-start.2 = (bf16[256,768]{1,0:T(8,128)(2,1)S(1)}, bf16[256,768]{1,0:T(8,128)(2,1)S(1)}, u32[]{:S(2)}, u32[]{:S(2)}) collective-permute-start(bf16[256,768]{1,0:T(8,128)(2,1)S(1)} %bitcast.19), channel_id=1, source_target_pairs={{0,24},{8,16},{16,8},{24,0},{1,25},{9,17},{17,9},{25,1},{2,26},{10... | collective-permute-start | bytes 1179656 | tf_op jit(solution)/shard_map/ppermute | solution.py:153
  13.1 23.8 %collective-permute-start.1 = (bf16[256,768]{1,0:T(8,128)(2,1)S(1)}, bf16[256,768]{1,0:T(8,128)(2,1)S(1)}, u32[]{:S(2)}, u32[]{:S(2)}) collective-permute-start(bf16[256,768]{1,0:T(8,128)(2,1)S(1)} %bitcast.20), channel_id=1, source_target_pairs={{0,16},{8,24},{16,0},{24,8},{1,17},{9,25},{17,1},{25,9},{2,18},{10... | collective-permute-start | bytes 1179656 | tf_op jit(solution)/shard_map/ppermute | solution.py:153
  13.6 23.3 %collective-permute-start = (bf16[256,768]{1,0:T(8,128)(2,1)S(1)}, bf16[256,768]{1,0:T(8,128)(2,1)S(1)}, u32[]{:S(2)}, u32[]{:S(2)}) collective-permute-start(bf16[256,768]{1,0:T(8,128)(2,1)S(1)} %bitcast.21), channel_id=1, source_target_pairs={{0,8},{8,0},{16,24},{24,16},{1,9},{9,1},{17,25},{25,17},{2,10},{10... | collective-permute-start | bytes 1179656 | tf_op jit(solution)/shard_map/ppermute | solution.py:153
  14.1 29.0 %collective-permute-start.9 = (bf16[256,768]{1,0:T(8,128)(2,1)S(1)}, bf16[256,768]{1,0:T(8,128)(2,1)S(1)}, u32[]{:S(2)}, u32[]{:S(2)}) collective-permute-start(bf16[256,768]{1,0:T(8,128)(2,1)S(1)} %bitcast.22), channel_id=1, source_target_pairs={{6,2},{7,3},{14,10},{15,11},{22,18},{23,19},{30,26},{31,27}} | collective-permute-start | bytes 1179656 | tf_op jit(solution)/shard_map/ppermute | solution.py:170
  33.4 29.8 %all-to-all-start.1 = ((bf16[4,256,256]{2,1,0:T(8,128)(2,1)}), bf16[4,256,256]{2,1,0:T(8,128)(2,1)S(1)}, u32[]{:S(2)}, u32[]{:S(2)}) async-start(bf16[4,256,256]{2,1,0:T(8,128)(2,1)} %get-tuple-element.9), calls=%async_computation.1 | async-start | bytes 1048576 | tf_op jit(solution)/shard_map/all_to_all | solution.py:181
  39.3 6.0 %collective-permute-start.3 = (bf16[256,256]{1,0:T(8,128)(2,1)S(1)}, bf16[256,256]{1,0:T(8,128)(2,1)S(1)}, u32[]{:S(2)}, u32[]{:S(2)}) collective-permute-start(bf16[256,256]{1,0:T(8,128)(2,1)S(1)} %shard_map.37), channel_id=1, source_target_pairs={{6,2},{7,3},{14,10},{15,11},{22,18},{23,19},{30,26},{31,27}} | collective-permute-start | bytes 393224 | tf_op jit(solution)/shard_map/ppermute | solution.py:170
  42.4 11.4 %collective-permute-start.16 = (bf16[256,512]{1,0:T(8,128)(2,1)S(1)}, bf16[256,512]{1,0:T(8,128)(2,1)S(1)}, u32[]{:S(2)}, u32[]{:S(2)}) collective-permute-start(bf16[256,512]{1,0:T(8,128)(2,1)S(1)} %shard_map.39), channel_id=1, source_target_pairs={{6,2},{7,3},{14,10},{15,11},{22,18},{23,19},{30,26},{31,27}} | collective-permute-start | bytes 786440 | tf_op jit(solution)/shard_map/ppermute | solution.py:170
  43.2 41.4 %copy-start.2 = (bf16[8,1,64,768]{3,2,1,0:T(8,128)(2,1)S(1)}, bf16[8,1,64,768]{3,2,1,0:T(8,128)(2,1)}, u32[]{:S(2)}) copy-start(bf16[8,1,64,768]{3,2,1,0:T(8,128)(2,1)} %param.4) | copy-start | bytes 2359300
  43.2 16.4 %collective-permute-start.11 = (bf16[256,768]{1,0:T(8,128)(2,1)S(1)}, bf16[256,768]{1,0:T(8,128)(2,1)S(1)}, u32[]{:S(2)}, u32[]{:S(2)}) collective-permute-start(bf16[256,768]{1,0:T(8,128)(2,1)S(1)} %broadcast_select_fusion), channel_id=1, source_target_pairs={{2,0},{3,1},{10,8},{11,9},{18,16},{19,17},{26,24},{27,25}} | collective-permute-start | bytes 1179656 | tf_op jit(solution)/shard_map/ppermute | solution.py:165
  44.6 15.0 %collective-permute-start.10 = (bf16[256,768]{1,0:T(8,128)(2,1)S(1)}, bf16[256,768]{1,0:T(8,128)(2,1)S(1)}, u32[]{:S(2)}, u32[]{:S(2)}) collective-permute-start(bf16[256,768]{1,0:T(8,128)(2,1)S(1)} %broadcast_select_fusion), channel_id=1, source_target_pairs={{2,4},{3,5},{10,12},{11,13},{18,20},{19,21},{26,28},{27,29}} | collective-permute-start | bytes 1179656 | tf_op jit(solution)/shard_map/ppermute | solution.py:164
  45.4 17.9 %collective-permute-start.4 = (bf16[256,256]{1,0:T(8,128)(2,1)S(1)}, bf16[256,256]{1,0:T(8,128)(2,1)}, u32[]{:S(2)}, u32[]{:S(2)}) collective-permute-start(bf16[256,256]{1,0:T(8,128)(2,1)S(1)} %broadcast_select_fusion.3), channel_id=1, source_target_pairs={{2,0},{6,4},{0,2},{4,6},{3,1},{7,5},{1,3},{5,7},{10,8},{14,12},{8,... | collective-permute-start | bytes 393224 | tf_op jit(solution)/shard_map/ppermute | solution.py:170
  53.8 12.6 %collective-permute-start.17 = (bf16[256,512]{1,0:T(8,128)(2,1)S(1)}, bf16[256,512]{1,0:T(8,128)(2,1)}, u32[]{:S(2)}, u32[]{:S(2)}) collective-permute-start(bf16[256,512]{1,0:T(8,128)(2,1)S(1)} %broadcast_select_fusion.1), channel_id=1, source_target_pairs={{2,0},{6,4},{0,2},{4,6},{3,1},{7,5},{1,3},{5,7},{10,8},{14,12},{8,... | collective-permute-start | bytes 786440 | tf_op jit(solution)/shard_map/ppermute | solution.py:170
  59.7 13.0 %collective-permute-start.14 = (bf16[256,768]{1,0:T(8,128)(2,1)S(1)}, bf16[256,768]{1,0:T(8,128)(2,1)S(1)}, u32[]{:S(2)}, u32[]{:S(2)}) collective-permute-start(bf16[256,768]{1,0:T(8,128)(2,1)S(1)} %select_select_fusion.refs_0_), channel_id=1, source_target_pairs={{0,24},{8,16},{16,8},{24,0},{1,25},{9,17},{17,9},{25,1},{2,26},{10... | collective-permute-start | bytes 1179656 | tf_op jit(solution)/shard_map/ppermute | solution.py:153
  62.2 17.9 %collective-permute-start.13 = (bf16[256,768]{1,0:T(8,128)(2,1)S(1)}, bf16[256,768]{1,0:T(8,128)(2,1)}, u32[]{:S(2)}, u32[]{:S(2)}) collective-permute-start(bf16[256,768]{1,0:T(8,128)(2,1)S(1)} %select_select_fusion.refs_0_), channel_id=1, source_target_pairs={{0,16},{8,24},{16,0},{24,8},{1,17},{9,25},{17,1},{25,9},{2,18},{10... | collective-permute-start | bytes 1179656 | tf_op jit(solution)/shard_map/ppermute | solution.py:153
  62.7 18.9 %collective-permute-start.12 = (bf16[256,768]{1,0:T(8,128)(2,1)S(1)}, bf16[256,768]{1,0:T(8,128)(2,1)}, u32[]{:S(2)}, u32[]{:S(2)}) collective-permute-start(bf16[256,768]{1,0:T(8,128)(2,1)S(1)} %select_select_fusion.refs_0_), channel_id=1, source_target_pairs={{0,8},{8,0},{16,24},{24,16},{1,9},{9,1},{17,25},{25,17},{2,10},{10... | collective-permute-start | bytes 1179656 | tf_op jit(solution)/shard_map/ppermute | solution.py:153
  63.2 20.1 %collective-permute-start.15 = (bf16[4,256,256]{2,1,0:T(8,128)(2,1)S(1)}, bf16[4,256,256]{2,1,0:T(8,128)(2,1)S(1)}, u32[]{:S(2)}, u32[]{:S(2)}) collective-permute-start(bf16[4,256,256]{2,1,0:T(8,128)(2,1)S(1)} %all-to-all-done.refs_5_), channel_id=1, source_target_pairs={{0,1},{1,0},{2,3},{3,2},{4,5},{5,4},{6,7},{7,6},{8,9},{9,8},{10,11... | collective-permute-start | bytes 1572872 | tf_op jit(solution)/shard_map/ppermute | solution.py:184
  66.4 25.0 %collective-permute-start.8 = (bf16[4,256,256]{2,1,0:T(8,128)(2,1)S(1)}, bf16[4,256,256]{2,1,0:T(8,128)(2,1)S(1)}, u32[]{:S(2)}, u32[]{:S(2)}) collective-permute-start(bf16[4,256,256]{2,1,0:T(8,128)(2,1)S(1)} %all-to-all-done.1.refs_5_), channel_id=1, source_target_pairs={{0,1},{1,0},{2,3},{3,2},{4,5},{5,4},{6,7},{7,6},{8,9},{9,8},{10,11... | collective-permute-start | bytes 1572872 | tf_op jit(solution)/shard_map/ppermute | solution.py:184
  72.6 20.4 %collective-permute-start.20 = (bf16[256,512]{1,0:T(8,128)(2,1)S(1)}, bf16[256,512]{1,0:T(8,128)(2,1)S(1)}, u32[]{:S(2)}, u32[]{:S(2)}) collective-permute-start(bf16[256,512]{1,0:T(8,128)(2,1)S(1)} %broadcast_select_fusion.2.refs_0_), channel_id=1, source_target_pairs={{0,24},{8,16},{16,8},{24,0},{1,25},{9,17},{17,9},{25,1},{2,26},{10... | collective-permute-start | bytes 786440 | tf_op jit(solution)/shard_map/ppermute | solution.py:153
  80.1 13.7 %collective-permute-start.19 = (bf16[256,512]{1,0:T(8,128)(2,1)S(1)}, bf16[256,512]{1,0:T(8,128)(2,1)S(1)}, u32[]{:S(2)}, u32[]{:S(2)}) collective-permute-start(bf16[256,512]{1,0:T(8,128)(2,1)S(1)} %broadcast_select_fusion.2.refs_0_), channel_id=1, source_target_pairs={{0,16},{8,24},{16,0},{24,8},{1,17},{9,25},{17,1},{25,9},{2,18},{10... | collective-permute-start | bytes 786440 | tf_op jit(solution)/shard_map/ppermute | solution.py:153
  81.6 12.2 %collective-permute-start.18 = (bf16[256,512]{1,0:T(8,128)(2,1)S(1)}, bf16[256,512]{1,0:T(8,128)(2,1)S(1)}, u32[]{:S(2)}, u32[]{:S(2)}) collective-permute-start(bf16[256,512]{1,0:T(8,128)(2,1)S(1)} %broadcast_select_fusion.2.refs_0_), channel_id=1, source_target_pairs={{0,8},{8,0},{16,24},{24,16},{1,9},{9,1},{17,25},{25,17},{2,10},{10... | collective-permute-start | bytes 786440 | tf_op jit(solution)/shard_map/ppermute | solution.py:153
  83.3 14.5 %collective-permute-start.7 = (bf16[256,256]{1,0:T(8,128)(2,1)S(1)}, bf16[256,256]{1,0:T(8,128)(2,1)S(1)}, u32[]{:S(2)}, u32[]{:S(2)}) collective-permute-start(bf16[256,256]{1,0:T(8,128)(2,1)S(1)} %broadcast_select_fusion.4.refs_0_), channel_id=1, source_target_pairs={{0,24},{8,16},{16,8},{24,0},{1,25},{9,17},{17,9},{25,1},{2,26},{10... | collective-permute-start | bytes 393224 | tf_op jit(solution)/shard_map/ppermute | solution.py:153
  91.4 6.4 %collective-permute-start.6 = (bf16[256,256]{1,0:T(8,128)(2,1)S(1)}, bf16[256,256]{1,0:T(8,128)(2,1)S(1)}, u32[]{:S(2)}, u32[]{:S(2)}) collective-permute-start(bf16[256,256]{1,0:T(8,128)(2,1)S(1)} %broadcast_select_fusion.4.refs_0_), channel_id=1, source_target_pairs={{0,16},{8,24},{16,0},{24,8},{1,17},{9,25},{17,1},{25,9},{2,18},{10... | collective-permute-start | bytes 393224 | tf_op jit(solution)/shard_map/ppermute | solution.py:153
  93.0 5.0 %collective-permute-start.5 = (bf16[256,256]{1,0:T(8,128)(2,1)S(1)}, bf16[256,256]{1,0:T(8,128)(2,1)S(1)}, u32[]{:S(2)}, u32[]{:S(2)}) collective-permute-start(bf16[256,256]{1,0:T(8,128)(2,1)S(1)} %broadcast_select_fusion.4.refs_0_), channel_id=1, source_target_pairs={{0,8},{8,0},{16,24},{24,16},{1,9},{9,1},{17,25},{25,17},{2,10},{10... | collective-permute-start | bytes 393224 | tf_op jit(solution)/shard_map/ppermute | solution.py:153
  (2 other events, 9.6 us)
